TPU v7x, 32 devices: a whole 2x2x4 slice. The times are simulated.
32 devices in a mesh: rows: 4 (over x, core), feat: 8 (over z, y).
Axes of the slice: x: 2, y: 2, z: 4, core: 2. Of those that a mesh axis runs over, the one named last changes fastest.
Arguments:
- embeddings: bfloat16 [512, 1024], P(('rows', 'feat')), may hold values from -12 to 12
- freqs: bfloat16 [1024, 65536], P(None, 'feat'), may hold values from -0.1875 to 0.1875
- phases: float32 [65536], P('feat'), may hold values from 0 to 6.2831855
- sketch: bfloat16 [65536, 256], P('feat'), may hold values from -0.0234375 to 0.0234375
Outputs:
- basis: float32 [512, 256], P(('rows', 'feat'))
- coeffs: float32 [256, 65536], P(None, 'feat')
All inputs are finite; a program needn't handle non-finite values.
Results may differ from a plain program's by a relative error of at most 0.0048.
Values may be sent and summed in bfloat16 or wider, within the bound.
A program may use at most 128 MiB of HBM per device.

v0:
```python
import jax
import jax.numpy as jnp
from jax import lax
from jax.sharding import PartitionSpec as P


def per_device(embeddings, freqs, phases, sketch):
    rows_dev = embeddings.shape[0]
    row_count = rows_dev * lax.axis_size("feat") * lax.axis_size("rows")
    mixed = jnp.dot(
        lax.all_gather(embeddings, "feat", axis=0, tiled=True),
        freqs,
        preferred_element_type=jnp.float32,
    )
    features = jnp.cos(mixed + phases).astype(jnp.bfloat16)
    owned_rows = lax.psum_scatter(
        jnp.dot(features, sketch, preferred_element_type=jnp.float32),
        "feat",
        scatter_dimension=0,
        tiled=True,
    )
    local_gram = jnp.dot(owned_rows.T, owned_rows, precision=lax.Precision.HIGHEST)
    gram_matrix = lax.psum(local_gram, ("rows", "feat")) / row_count
    factor = jnp.linalg.cholesky(gram_matrix)
    basis = jax.scipy.linalg.solve_triangular(factor, owned_rows.T, lower=True).T
    block_basis = lax.all_gather(basis.astype(jnp.bfloat16), "feat", axis=0, tiled=True)
    partial_value = lax.dot_general(
        block_basis, features, (((0,), (0,)), ((), ())), preferred_element_type=jnp.float32
    )
    coeffs = lax.psum(partial_value, "rows") / row_count
    return (basis, coeffs)


def solution(mesh):
    placed = (P(("rows", "feat"), None), P(None, "feat"), P("feat"), P("feat", None))
    return jax.shard_map(
        per_device,
        mesh=mesh,
        in_specs=placed,
        out_specs=(P(("rows", "feat"), None), P(None, "feat")),
        check_vma=False,
    )
```

profile of v0, /device:TPU:0, one launch (start us, length us, event | category | flops | bytes accessed | tf_op | source)
XLA Modules:
  0.0 516.5 jit_solution(3243274491165157878)
XLA Ops:
  7.2 32.7 %all_gather.6 = bf16[128,1024]{1,0:T(8,128)(2,1)S(1)} all-gather(bf16[16,1024]{1,0:T(8,128)(2,1)} %param.4), channel_id=1, replica_groups=mesh['rows'=4,'feat'=8] {'feat'}, dimensions={0}, use_global_device_ids=true | all-gather | bytes 294912 | tf_op jit(solution)/shard_map/all_gather | solution.py:11
  40.0 18.1 %fusion.1 = bf16[128,8192]{1,0:T(8,128)(2,1)S(1)} fusion(bf16[128,1024]{1,0:T(8,128)(2,1)S(1)} %all_gather.6, bf16[1024,8192]{1,0:T(8,128)(2,1)} %param.5, f32[8192]{0:T(1024)} %param.6), kind=kOutput, calls=%fused_computation.4 | convolution fusion | flops 2149580800 | bytes 19169280 | tf_op jit(solution)/shard_map/dot_general | solution.py:10
  58.1 1.5 fusion.12
  59.6 0.0 all-reduce.4.cloned.1.call-start
  59.6 62.0 %reduce-scatter.2.cloned.1.call-done = f32[16,256]{1,0:T(8,128)} async-done(((f32[128,256]{1,0:T(8,128)}), f32[16,256]{1,0:T(8,128)}) %reduce-scatter.2.cloned.1.call-update) | async-done | bytes 16400 | tf_op jit(solution)/shard_map/reduce_scatter | solution.py:16
  121.6 1.9 fusion.13
  123.6 0.2 all-reduce.6.cloned.1.call-start
  123.8 128.0 %all-reduce.4.cloned.1.call-done = f32[256,256]{0,1:T(8,128)} async-done(((f32[256,256]{0,1:T(8,128)}), f32[256,256]{0,1:T(8,128)}) %all-reduce.4.cloned.1.call-update) | async-done | bytes 262160 | tf_op jit(solution)/shard_map/psum | solution.py:23
  251.8 1.0 broadcast_multiply_fusion.1
  252.8 0.1 copy.7
  252.9 1.0 fusion.2
  253.9 11.7 %cholesky.50 = f32[128,128]{1,0:T(8,128)S(1)} custom-call(f32[128,128]{1,0:T(8,128)S(1)} %cholesky.118), custom_call_target="Cholesky" | custom-call | tf_op jit(solution)/shard_map/jit(cholesky)/cholesky | solution.py:24
  265.7 9.8 %custom-call.15 = f32[1,128,128]{1,2,0:T(8,128)S(1)} custom-call(f32[1,128,128]{2,1,0:T(8,128)S(1)} %get-tuple-element.25), custom_call_target="InvertDiagBlocksLowerTriangular" | custom-call | tf_op jit(solution)/shard_map/jit(cholesky)/cholesky | solution.py:24
  275.5 0.2 constant_dynamic-update-slice_fusion.1
  275.7 0.3 convolution_subtract_fusion
  276.0 11.7 %cholesky.105 = f32[128,128]{1,0:T(8,128)S(1)} custom-call(f32[128,128]{1,0:T(8,128)S(1)} %convolution_subtract_fusion), custom_call_target="Cholesky" | custom-call | tf_op jit(solution)/shard_map/jit(cholesky)/cholesky | solution.py:24
  287.8 0.7 compare_reduce_fusion
  289.9 0.1 triangular_solve.57
  289.9 4.3 while.1
  290.1 0.6 fusion.28
  290.7 1.4 bitcast_dynamic-update-slice_fusion.2
  292.2 0.6 fusion.28
  292.8 1.4 bitcast_dynamic-update-slice_fusion.2
  294.2 19.7 %custom-call.16 = f32[2,128,128]{1,2,0:T(8,128)S(1)} custom-call(f32[2,128,128]{2,1,0:T(8,128)S(1)} %get-tuple-element.9), custom_call_target="InvertDiagBlocksLowerTriangular" | custom-call | tf_op jit(solution)/shard_map/jit(_solve_triangular)/triangular_solve | solution.py:25
  313.9 0.2 fusion.5
  314.1 0.2 convolution_subtract_fusion.1
  314.3 0.2 fusion.4
  314.5 0.6 fusion.10
  315.1 30.5 %all_gather.7 = bf16[128,256]{1,0:T(8,128)(2,1)S(1)} all-gather(bf16[16,256]{1,0:T(8,128)(2,1)S(1)} %get-tuple-element.18), channel_id=1, replica_groups=mesh['rows'=4,'feat'=8] {'feat'}, dimensions={0}, use_global_device_ids=true | all-gather | bytes 73728 | tf_op jit(solution)/shard_map/all_gather | solution.py:26
  345.6 4.7 fusion.14
  350.3 152.0 %all-reduce.6.cloned.1.call-done = f32[256,8192]{1,0:T(8,128)} async-done(((f32[256,8192]{1,0:T(8,128)}), f32[256,8192]{1,0:T(8,128)}) %all-reduce.6.cloned.1.call-update) | async-done | bytes 8388624 | tf_op jit(solution)/shard_map/psum | solution.py:30
  502.3 7.7 %broadcast_multiply_fusion = f32[256,8192]{1,0:T(8,128)} fusion(f32[256,8192]{1,0:T(8,128)} %all-reduce.6.cloned.1.call-done), kind=kLoop, calls=%fused_computation.5 | loop fusion | flops 2097152 | bytes 16777216 | tf_op jit(solution)/shard_map/div | solution.py:30
  (17 shorter events, 0.2 us)
Async XLA Ops:
  7.2 114.5 %reduce-scatter.2.cloned.1.call-start = ((), (), s32[]{:S(2)}) async-start(), calls=%async_computation.1 | async-start | bytes 147456 | tf_op jit(solution)/shard_map/reduce_scatter | solution.py:16
  39.9 18.2 %copy-start = (bf16[8192,256]{1,0:T(8,128)(2,1)S(1)}, bf16[8192,256]{1,0:T(8,128)(2,1)}, u32[]{:S(2)}) copy-start(bf16[8192,256]{1,0:T(8,128)(2,1)} %param.7) | copy-start | bytes 12582916
  59.6 192.2 %all-reduce.4.cloned.1.call-start = ((), (), s32[]{:S(2)}) async-start(), calls=%async_computation.2 | async-start | bytes 524288 | tf_op jit(solution)/shard_map/psum | solution.py:23
  121.6 192.3 %copy-start.1 = (f32[16,256]{1,0:T(8,128)S(1)}, f32[16,256]{1,0:T(8,128)}, u32[]{:S(2)}) copy-start(f32[16,256]{1,0:T(8,128)} %reduce-scatter.2.cloned.1.call-done) | copy-start | bytes 49156
  123.6 378.7 %all-reduce.6.cloned.1.call-start = ((), (), s32[]{:S(2)}) async-start(), calls=%async_computation.3 | async-start | bytes 16777216 | tf_op jit(solution)/shard_map/psum | solution.py:30
Sparse Core Ops, SparseCore 0:
  59.7 61.8 reduce-scatter.1
  127.7 124.0 all-reduce.3
  350.4 151.8 all-reduce.5
where the time goes:
time: 517 us
  waiting for transfers between devices  342 us (66%)
  other arithmetic  64 us (12%)
  blocking collectives  63.2 us (12%)
  matrix products  27.2 us (5%)
  between operations  15.2 us (3%)
    psum x1, waiting for transfers between devices, per_device(): coeffs = lax.psum(partial_value, 'rows') / row_count  152 us
    psum x1, waiting for transfers between devices, per_device(): gram_matrix = lax.psum(local_gram, ('rows', 'feat')) / row_count  128 us
    reduce_scatter x1, waiting for transfers between devices, per_device(): lax.psum_scatter(jnp.dot(features, sketch, preferred_element_type=jnp.flo...  62 us
    another operation x6, other arithmetic, per_device(): factor = jnp.linalg.cholesky(gram_matrix)  34 us
    all_gather x1, blocking collectives, per_device(): lax.all_gather(embeddings, 'feat', axis=0, tiled=True)  32.7 us
    all_gather x1, blocking collectives, per_device(): lax.all_gather(basis.astype(jnp.bfloat16), 'feat', axis=0, tiled=True)  30.5 us
    another operation x3, other arithmetic, per_device(): jax.scipy.linalg.solve_triangular(factor, owned_rows.T, lower=True)  19.7 us
    dot_general x1, matrix products, per_device(): jnp.dot(lax.all_gather(embeddings, 'feat', axis=0, tiled=True), freqs, pr...  18.1 us
  transfers between devices with their start and end apart: 3, of which 3 were waited for; matrix products, arithmetic and copies ran while one was open for 0% of the time, Pallas kernels for 0%

commit v1 on v0

--- a/solution.py
+++ b/solution.py
@@ -5,13 +5,41 @@
 
 
 def per_device(embeddings, freqs, phases, sketch):
+
+    def detail_works(field_in, mesh_dim, out_dim):
+        reply, even, upper = (
+            jax.lax.psum(1, mesh_dim),
+            jax.lax.axis_index(mesh_dim),
+            field_in.shape[out_dim],
+        )
+        rows = []
+        for it, hop_no in enumerate(field_in.shape):
+            rows.append(hop_no * reply if it == out_dim else hop_no)
+        odd = lax.dynamic_update_slice_in_dim(
+            jnp.zeros(rows, field_in.dtype), field_in, even * upper, axis=out_dim
+        )
+        e_next = outcome_arr = field_in
+        for kk in range(1, reply // 2 + 1):
+            made = []
+            for it in range(reply):
+                made.append((it, (it + 1) % reply))
+            e_next = jax.lax.ppermute(e_next, mesh_dim, made)
+            odd = lax.dynamic_update_slice_in_dim(
+                odd, e_next, (even - kk) % reply * upper, axis=out_dim
+            )
+            if 2 * kk < reply:
+                history = []
+                for it in range(reply):
+                    history.append((it, (it - 1) % reply))
+                outcome_arr = jax.lax.ppermute(outcome_arr, mesh_dim, history)
+                odd = lax.dynamic_update_slice_in_dim(
+                    odd, outcome_arr, (even + kk) % reply * upper, axis=out_dim
+                )
+        return odd
+
     rows_dev = embeddings.shape[0]
     row_count = rows_dev * lax.axis_size("feat") * lax.axis_size("rows")
-    mixed = jnp.dot(
-        lax.all_gather(embeddings, "feat", axis=0, tiled=True),
-        freqs,
-        preferred_element_type=jnp.float32,
-    )
+    mixed = jnp.dot(detail_works(embeddings, "feat", 0), freqs, preferred_element_type=jnp.float32)
     features = jnp.cos(mixed + phases).astype(jnp.bfloat16)
     owned_rows = lax.psum_scatter(
         jnp.dot(features, sketch, preferred_element_type=jnp.float32),

time: 517 us -> 513 us (level)
  blocking collectives: 63.2 us -> 30.5 us
  starting transfers between devices: 0.3 us -> 16.3 us
  waiting for transfers between devices: 342 us -> 354 us
    all_gather x1 -> x0, blocking collectives: 32.7 us -> none  [per_device(): lax.all_gather(embeddings, 'feat', axis=0, tiled=True)]
    ppermute x0 -> x7, starting transfers between devices: none -> 16 us  [the longest x3 16 us: detail_works(): outcome_arr = jax.lax.ppermute(outcome_arr, mesh_dim, history)]
    ppermute x0 -> x7, waiting for transfers between devices: none -> 15.8 us  [the longest x4 13.2 us: detail_works(): e_next = jax.lax.ppermute(e_next, mesh_dim, made)]
  transfers between devices with their start and end apart: 3 -> 10, of which waited for: 3 -> 7; matrix products, arithmetic and copies ran while one was open for 0% -> 0% of each run, Pallas kernels for 0% -> 0%
where the time goes in v1:
time: 513 us; the launch traced here: 512 us
  waiting for transfers between devices  354 us (69%)
  other arithmetic  64 us (12%)
  blocking collectives  30.5 us (6%)
  matrix products  27.2 us (5%)
  starting transfers between devices  16.3 us (3%)
  between operations  15.2 us (3%)
    psum x1, waiting for transfers between devices, per_device(): coeffs = lax.psum(partial_value, 'rows') / row_count  152 us
    psum x1, waiting for transfers between devices, per_device(): gram_matrix = lax.psum(local_gram, ('rows', 'feat')) / row_count  128 us
    reduce_scatter x1, waiting for transfers between devices, per_device(): lax.psum_scatter(jnp.dot(features, sketch, preferred_element_type=jnp.flo...  58.3 us
    another operation x6, other arithmetic, per_device(): factor = jnp.linalg.cholesky(gram_matrix)  34 us
    all_gather x1, blocking collectives, per_device(): lax.all_gather(basis.astype(jnp.bfloat16), 'feat', axis=0, tiled=True)  30.5 us
    another operation x3, other arithmetic, per_device(): jax.scipy.linalg.solve_triangular(factor, owned_rows.T, lower=True)  19.7 us
    dot_general x1, matrix products, per_device(): jnp.dot(detail_works(embeddings, 'feat', 0), freqs, preferred_element_typ...  18.1 us
    ppermute x3, starting transfers between devices, detail_works(): outcome_arr = jax.lax.ppermute(outcome_arr, mesh_dim, history)  16 us
  transfers between devices with their start and end apart: 10, of which 7 were waited for; matrix products, arithmetic and copies ran while one was open for 0% of the time, Pallas kernels for 0%

profile of v1, /device:TPU:0, one launch (start us, length us, event | category | flops | bytes accessed | tf_op | source)
XLA Modules:
  0.0 512.4 jit_solution(13264872398807829216)
XLA Ops:
  7.2 6.1 %collective-permute-start.1 = (bf16[16,1024]{1,0:T(8,128)(2,1)}, bf16[16,1024]{1,0:T(8,128)(2,1)S(1)}, u32[]{:S(2)}, u32[]{:S(2)}) collective-permute-start(bf16[16,1024]{1,0:T(8,128)(2,1)} %param.4), channel_id=1, source_target_pairs={{0,7},{1,0},{2,1},{3,2},{4,3},{5,4},{6,5},{7,6},{8,15},{9,8},{10,9... | collective-permute-start | bytes 98312 | tf_op jit(solution)/shard_map/ppermute | solution.py:34
  13.3 0.8 constant_dynamic-update-slice_fusion.8
  14.1 1.1 collective-permute-done.1
  15.2 4.9 collective-permute-start.3
  20.1 1.6 collective-permute-done.3
  21.7 5.0 collective-permute-start.5
  26.7 6.6 %collective-permute-done.4 = bf16[16,1024]{1,0:T(8,128)(2,1)S(1)} collective-permute-done((bf16[16,1024]{1,0:T(8,128)(2,1)S(1)}, bf16[16,1024]{1,0:T(8,128)(2,1)S(1)}, u32[]{:S(2)}, u32[]{:S(2)}) %collective-permute-start.4) | collective-permute-done | bytes 32800 | tf_op jit(solution)/shard_map/ppermute | solution.py:26
  33.4 6.6 %collective-permute-done.6 = bf16[16,1024]{1,0:T(8,128)(2,1)S(1)} collective-permute-done((bf16[16,1024]{1,0:T(8,128)(2,1)S(1)}, bf16[16,1024]{1,0:T(8,128)(2,1)S(1)}, u32[]{:S(2)}, u32[]{:S(2)}) %collective-permute-start.6) | collective-permute-done | bytes 32800 | tf_op jit(solution)/shard_map/ppermute | solution.py:26
  39.9 18.1 %fusion.1 = bf16[128,8192]{1,0:T(8,128)(2,1)S(1)} fusion(bf16[128,1024]{1,0:T(8,128)(2,1)S(1)} %constant_dynamic-update-slice_fusion.1, bf16[1024,8192]{1,0:T(8,128)(2,1)} %param.5, f32[8192]{0:T(1024)} %param.6), kind=kOutput, calls=%fused_computation.4 | convolution fusion | flops 2149580800 | bytes 19169280 | tf_op jit(solution)/shard_map/dot_general | solution.py:42
  58.1 1.5 fusion.12
  59.6 58.3 %reduce-scatter.2.cloned.1.call-done = f32[16,256]{1,0:T(8,128)} async-done(((f32[128,256]{1,0:T(8,128)}), f32[16,256]{1,0:T(8,128)}) %reduce-scatter.2.cloned.1.call-update) | async-done | bytes 16400 | tf_op jit(solution)/shard_map/reduce_scatter | solution.py:44
  117.9 1.9 fusion.13
  119.9 0.2 all-reduce.6.cloned.1.call-start
  120.1 127.9 %all-reduce.4.cloned.1.call-done = f32[256,256]{0,1:T(8,128)} async-done(((f32[256,256]{0,1:T(8,128)}), f32[256,256]{0,1:T(8,128)}) %all-reduce.4.cloned.1.call-update) | async-done | bytes 262160 | tf_op jit(solution)/shard_map/psum | solution.py:51
  248.0 1.0 broadcast_multiply_fusion.1
  249.1 1.0 fusion.2
  250.1 11.7 %cholesky.50 = f32[128,128]{1,0:T(8,128)S(1)} custom-call(f32[128,128]{1,0:T(8,128)S(1)} %cholesky.118), custom_call_target="Cholesky" | custom-call | tf_op jit(solution)/shard_map/jit(cholesky)/cholesky | solution.py:52
  261.9 9.8 %custom-call.15 = f32[1,128,128]{1,2,0:T(8,128)S(1)} custom-call(f32[1,128,128]{2,1,0:T(8,128)S(1)} %get-tuple-element.25), custom_call_target="InvertDiagBlocksLowerTriangular" | custom-call | tf_op jit(solution)/shard_map/jit(cholesky)/cholesky | solution.py:52
  271.9 0.3 convolution_subtract_fusion
  272.2 11.7 %cholesky.105 = f32[128,128]{1,0:T(8,128)S(1)} custom-call(f32[128,128]{1,0:T(8,128)S(1)} %convolution_subtract_fusion), custom_call_target="Cholesky" | custom-call | tf_op jit(solution)/shard_map/jit(cholesky)/cholesky | solution.py:52
  283.9 0.7 compare_reduce_fusion
  286.0 4.1 while.1
  286.2 0.6 fusion.28
  286.8 1.4 bitcast_dynamic-update-slice_fusion.2
  288.1 0.6 fusion.28
  288.7 1.4 bitcast_dynamic-update-slice_fusion.2
  290.1 19.7 %custom-call.16 = f32[2,128,128]{1,2,0:T(8,128)S(1)} custom-call(f32[2,128,128]{2,1,0:T(8,128)S(1)} %get-tuple-element.9), custom_call_target="InvertDiagBlocksLowerTriangular" | custom-call | tf_op jit(solution)/shard_map/jit(_solve_triangular)/triangular_solve | solution.py:53
  310.3 0.6 fusion.10
  311.0 30.5 %all_gather.3 = bf16[128,256]{1,0:T(8,128)(2,1)S(1)} all-gather(bf16[16,256]{1,0:T(8,128)(2,1)S(1)} %get-tuple-element.18), channel_id=1, replica_groups=mesh['rows'=4,'feat'=8] {'feat'}, dimensions={0}, use_global_device_ids=true | all-gather | bytes 73728 | tf_op jit(solution)/shard_map/all_gather | solution.py:54
  341.5 4.7 fusion.14
  346.2 152.0 %all-reduce.6.cloned.1.call-done = f32[256,8192]{1,0:T(8,128)} async-done(((f32[256,8192]{1,0:T(8,128)}), f32[256,8192]{1,0:T(8,128)}) %all-reduce.6.cloned.1.call-update) | async-done | bytes 8388624 | tf_op jit(solution)/shard_map/psum | solution.py:58
  498.2 7.7 %broadcast_multiply_fusion = f32[256,8192]{1,0:T(8,128)} fusion(f32[256,8192]{1,0:T(8,128)} %all-reduce.6.cloned.1.call-done), kind=kLoop, calls=%fused_computation.5 | loop fusion | flops 2097152 | bytes 16777216 | tf_op jit(solution)/shard_map/div | solution.py:58
  (39 shorter events, 1.3 us)
Async XLA Ops:
  7.2 110.7 %reduce-scatter.2.cloned.1.call-start = ((), (), s32[]{:S(2)}) async-start(), calls=%async_computation.1 | async-start | bytes 147456 | tf_op jit(solution)/shard_map/reduce_scatter | solution.py:44
  7.2 8.0 %collective-permute-start.1 = (bf16[16,1024]{1,0:T(8,128)(2,1)}, bf16[16,1024]{1,0:T(8,128)(2,1)S(1)}, u32[]{:S(2)}, u32[]{:S(2)}) collective-permute-start(bf16[16,1024]{1,0:T(8,128)(2,1)} %param.4), channel_id=1, source_target_pairs={{0,7},{1,0},{2,1},{3,2},{4,3},{5,4},{6,5},{7,6},{8,15},{9,8},{10,9... | collective-permute-start | bytes 98312 | tf_op jit(solution)/shard_map/ppermute | solution.py:34
  13.3 6.8 %collective-permute-start = (bf16[16,1024]{1,0:T(8,128)(2,1)}, bf16[16,1024]{1,0:T(8,128)(2,1)S(1)}, u32[]{:S(2)}, u32[]{:S(2)}) collective-permute-start(bf16[16,1024]{1,0:T(8,128)(2,1)} %param.4), channel_id=1, source_target_pairs={{0,1},{1,2},{2,3},{3,4},{4,5},{5,6},{6,7},{7,0},{8,9},{9,10},{10,1... | collective-permute-start | bytes 98312 | tf_op jit(solution)/shard_map/ppermute | solution.py:26
  15.2 6.5 %collective-permute-start.3 = (bf16[16,1024]{1,0:T(8,128)(2,1)S(1)}, bf16[16,1024]{1,0:T(8,128)(2,1)S(1)}, u32[]{:S(2)}, u32[]{:S(2)}) collective-permute-start(bf16[16,1024]{1,0:T(8,128)(2,1)S(1)} %collective-permute-done.1), channel_id=1, source_target_pairs={{0,7},{1,0},{2,1},{3,2},{4,3},{5,4},{6,5},{7,6},{8,15},{9,8},{10,9... | collective-permute-start | bytes 98312 | tf_op jit(solution)/shard_map/ppermute | solution.py:34
  20.1 6.6 %collective-permute-start.2 = (bf16[16,1024]{1,0:T(8,128)(2,1)S(1)}, bf16[16,1024]{1,0:T(8,128)(2,1)S(1)}, u32[]{:S(2)}, u32[]{:S(2)}) collective-permute-start(bf16[16,1024]{1,0:T(8,128)(2,1)S(1)} %collective-permute-done), channel_id=1, source_target_pairs={{0,1},{1,2},{2,3},{3,4},{4,5},{5,6},{6,7},{7,0},{8,9},{9,10},{10,1... | collective-permute-start | bytes 98312 | tf_op jit(solution)/shard_map/ppermute | solution.py:26
  21.7 11.6 %collective-permute-start.5 = (bf16[16,1024]{1,0:T(8,128)(2,1)S(1)}, bf16[16,1024]{1,0:T(8,128)(2,1)S(1)}, u32[]{:S(2)}, u32[]{:S(2)}) collective-permute-start(bf16[16,1024]{1,0:T(8,128)(2,1)S(1)} %collective-permute-done.3), channel_id=1, source_target_pairs={{0,7},{1,0},{2,1},{3,2},{4,3},{5,4},{6,5},{7,6},{8,15},{9,8},{10,9... | collective-permute-start | bytes 98312 | tf_op jit(solution)/shard_map/ppermute | solution.py:34
  26.7 6.6 %collective-permute-start.4 = (bf16[16,1024]{1,0:T(8,128)(2,1)S(1)}, bf16[16,1024]{1,0:T(8,128)(2,1)S(1)}, u32[]{:S(2)}, u32[]{:S(2)}) collective-permute-start(bf16[16,1024]{1,0:T(8,128)(2,1)S(1)} %collective-permute-done.2), channel_id=1, source_target_pairs={{0,1},{1,2},{2,3},{3,4},{4,5},{5,6},{6,7},{7,0},{8,9},{9,10},{10,1... | collective-permute-start | bytes 98312 | tf_op jit(solution)/shard_map/ppermute | solution.py:26
  33.3 6.6 %collective-permute-start.6 = (bf16[16,1024]{1,0:T(8,128)(2,1)S(1)}, bf16[16,1024]{1,0:T(8,128)(2,1)S(1)}, u32[]{:S(2)}, u32[]{:S(2)}) collective-permute-start(bf16[16,1024]{1,0:T(8,128)(2,1)S(1)} %collective-permute-done.4), channel_id=1, source_target_pairs={{0,1},{1,2},{2,3},{3,4},{4,5},{5,6},{6,7},{7,0},{8,9},{9,10},{10,1... | collective-permute-start | bytes 98312 | tf_op jit(solution)/shard_map/ppermute | solution.py:26
  39.9 18.2 %copy-start = (bf16[8192,256]{1,0:T(8,128)(2,1)S(1)}, bf16[8192,256]{1,0:T(8,128)(2,1)}, u32[]{:S(2)}) copy-start(bf16[8192,256]{1,0:T(8,128)(2,1)} %param.7) | copy-start | bytes 12582916
  59.6 188.4 %all-reduce.4.cloned.1.call-start = ((), (), s32[]{:S(2)}) async-start(), calls=%async_computation.2 | async-start | bytes 524288 | tf_op jit(solution)/shard_map/psum | solution.py:51
  117.9 191.9 %copy-start.1 = (f32[16,256]{1,0:T(8,128)S(1)}, f32[16,256]{1,0:T(8,128)}, u32[]{:S(2)}) copy-start(f32[16,256]{1,0:T(8,128)} %reduce-scatter.2.cloned.1.call-done) | copy-start | bytes 49156
  119.9 378.3 %all-reduce.6.cloned.1.call-start = ((), (), s32[]{:S(2)}) async-start(), calls=%async_computation.3 | async-start | bytes 16777216 | tf_op jit(solution)/shard_map/psum | solution.py:58
Sparse Core Ops, SparseCore 0:
  59.7 58.1 reduce-scatter.1
  124.0 123.9 all-reduce.3
  346.3 151.8 all-reduce.5
